TPU v7x, 128 devices: a whole 4x4x4 slice. The times are simulated.
128 devices in a mesh: dom: 8 (over x, core), blk: 16 (over z, y).
Axes of the slice: x: 4, y: 4, z: 4, core: 2. Of those that a mesh axis runs over, the one named last changes fastest.
Arguments:
- incident: bfloat16 [1024, 512, 192], P(('dom', 'blk')), may hold values from -6 to 6
- t_matrices: bfloat16 [1024, 512, 512], P(('dom', 'blk')), may hold values from -0.25 to 0.25
- translations: bfloat16 [4, 512, 512], replicated, may hold values from -0.125 to 0.125
- near_index: int32 [1024, 6], P(('dom', 'blk')), may hold values from 0 to 1023, as said below
- near_count: int32 [1024], P(('dom', 'blk')), may hold values from 1 to 6, as said below
- near_type: int32 [1024, 6], P(('dom', 'blk')), may hold values from 0 to 3
- phases: bfloat16 [1024, 2048], P(('dom', 'blk')), may hold values from -1 to 1
- wave_basis: bfloat16 [2048, 512], replicated, may hold values from -0.25 to 0.25
- grating_blocks: float32 [16, 128, 128], P('blk'), may hold values from -0.01171875 to 0.01171875
Outputs:
- coeffs: bfloat16 [1024, 512, 192], P(('dom', 'blk'))
Inputs may be any that keep to these rules, and one draw needn't show every extreme that they name: `near_index`: the first near_count[p] entries of row p are distinct particles other than p, each within 4 of p, ascending; the remaining entries equal p and carry no weight. `near_count`: some particle has exactly 6 live neighbours.
All inputs are finite; a program needn't handle non-finite values.
Results may differ from a plain program's by a relative error of at most 0.015.
Values may be sent and summed in bfloat16 or wider, within the bound.
A program may use at most 64 MiB of HBM per device.

v0:
```python
import jax
import jax.numpy as jnp
from jax import lax
from jax.sharding import PartitionSpec as P

ITERS = 2


def padded(array, sides, width):
    for axis, dim in sides:
        peers, length = (lax.axis_size(axis), array.shape[dim])
        up = [(i, (i + 1) % peers) for i in range(peers - 1)]
        down = [(j, i) for i, j in up]
        last = lax.slice_in_dim(array, length - width, length, axis=dim)
        initial = lax.slice_in_dim(array, 0, width, axis=dim)
        before = lax.ppermute(last, axis, up)
        after = lax.ppermute(initial, axis, down)
        array = jnp.concatenate([before, array, after], axis=dim)
    return array


def local(
    incident,
    t_matrices,
    translations,
    near_index,
    near_count,
    near_type,
    phases,
    wave_basis,
    grating_blocks,
):
    local_count = incident.shape[0]
    reach = local_count // 2
    kinds = translations.shape[0]
    most = near_index.shape[1]
    total_rows = wave_basis.shape[0]
    block_rows = total_rows // lax.axis_size("blk")
    order = grating_blocks.shape[1]
    first_index = lax.axis_index(("dom", "blk")) * local_count
    slots = near_index - first_index + reach
    live = jnp.arange(most)[None, :] < near_count[:, None]
    kind_hit = (near_type[None] == jnp.arange(kinds)[:, None, None]) & live[None]
    place_hit = slots[:, :, None] == jnp.arange(local_count + 2 * reach)[None, None, :]
    selector = jnp.sum((kind_hit[..., None] & place_hit[None]).astype(jnp.float32), axis=2).astype(
        jnp.bfloat16
    )
    phase_wide = phases.astype(jnp.float32)

    def scatter_solve(source):
        return jnp.einsum(
            "pab,pbm->pam", t_matrices, source, preferred_element_type=jnp.float32
        ).astype(jnp.bfloat16)

    coeffs = scatter_solve(incident)
    for sweep in range(ITERS):
        current = coeffs
        extended = padded(current, ((("dom", "blk"), 0),), reach)
        grouped = jnp.einsum(
            "tij,jlm->tilm", selector, extended, preferred_element_type=jnp.float32
        ).astype(jnp.bfloat16)
        near_field = jnp.einsum(
            "tab,tibm->iam", translations, grouped, preferred_element_type=jnp.float32
        )
        spread = jnp.einsum("gl,plm->pgm", wave_basis, current, preferred_element_type=jnp.float32)
        partial_rows = lax.psum_scatter(
            jnp.einsum("pg,pgm->gm", phase_wide, spread).astype(jnp.bfloat16),
            "blk",
            scatter_dimension=0,
            tiled=True,
        )
        sums = lax.psum_scatter(partial_rows, "dom", scatter_dimension=1, tiled=True).astype(
            jnp.float32
        )
        columns = sums.shape[1]
        shaped = sums.reshape(grating_blocks.shape[0], order, columns)
        result = jnp.einsum("bij,bjm->bim", grating_blocks, shaped, precision=lax.Precision.HIGHEST)
        reflected = lax.all_gather(
            result.reshape(block_rows, columns).astype(jnp.bfloat16), "dom", axis=1, tiled=True
        )
        weighted = (
            phase_wide[:, :, None]
            * lax.all_gather(reflected, "blk", axis=0, tiled=True).astype(jnp.float32)[None]
        ).astype(jnp.bfloat16)
        returned = jnp.einsum(
            "gl,pgm->plm", wave_basis, weighted, preferred_element_type=jnp.float32
        )
        source = (incident.astype(jnp.float32) + near_field + returned).astype(jnp.bfloat16)
        coeffs = scatter_solve(source)
    return coeffs


def solution(mesh):
    placed = (
        P(("dom", "blk"), None, None),
        P(("dom", "blk"), None, None),
        P(),
        P(("dom", "blk"), None),
        P(("dom", "blk")),
        P(("dom", "blk"), None),
        P(("dom", "blk"), None),
        P(),
        P("blk", None, None),
    )
    return jax.shard_map(
        local, mesh=mesh, in_specs=placed, out_specs=P(("dom", "blk"), None, None), check_vma=False
    )
```

profile of v0, /device:TPU:0, one launch (start us, length us, event | category | flops | bytes accessed | tf_op | source)
XLA Modules:
  0.0 359.9 jit_solution(5381657123738965866)
XLA Ops:
  6.5 4.3 %convolution_convert_fusion.4 = bf16[8,512,192]{1,2,0:T(8,128)(2,1)S(1)} fusion(bf16[8,512,512]{2,1,0:T(8,128)(2,1)} %param.10, bf16[8,512,192]{1,2,0:T(8,128)(2,1)} %param.9), kind=kOutput, calls=%fused_computation.38 | convolution fusion | flops 806092800 | bytes 7340032 | tf_op jit(solution)/shard_map/pab,pbm->pam/dot_general | solution.py:51
  10.9 0.0 copy-start.1
  10.9 1.5 fusion.66
  12.4 3.6 %collective-permute-start = (bf16[4,512,192]{1,2,0:T(8,128)(2,1)}, bf16[4,512,192]{1,2,0:T(8,128)(2,1)S(1)}, u32[]{:S(2)}, u32[]{:S(2)}) collective-permute-start(bf16[4,512,192]{1,2,0:T(8,128)(2,1)} %get-tuple-element.7), channel_id=1, source_target_pairs={{0,1},{1,2},{2,3},{3,4},{4,5},{5,6},{6,7},{7,8},{8,9},{9,10},{10,1... | collective-permute-start | bytes 2359304 | tf_op jit(solution)/shard_map/ppermute | solution.py:16
  16.0 1.3 collective-permute-start.1
  17.4 0.0 copy-start.5
  17.4 0.0 copy-start.8
  17.4 4.8 %fusion.1 = bf16[2048,192]{0,1:T(8,128)(2,1)} fusion(f32[2048,8]{0,1:T(8,128)S(1)} %get-tuple-element.10, bf16[8,512,192]{1,2,0:T(8,128)(2,1)S(1)} %convolution_convert_fusion.4, bf16[2048,512]{1,0:T(8,128)(2,1)S(1)} %copy-done), kind=kOutput, calls=%fused_computation.3 | convolution fusion | flops 3227123712 | bytes 4521984 | tf_op jit(solution)/shard_map/gl,plm->pgm/dot_general | solution.py:65
  22.2 2.2 copy.27
  24.4 0.0 reduce-scatter.5.cloned.1.call-update
  24.4 0.0 reduce-scatter.7.cloned.1.call-start
  24.5 0.1 copy.13
  24.6 0.1 copy.12
  24.7 0.7 dynamic-slice
  26.1 0.1 iota_compare_fusion
  26.1 0.1 convert_reduce_fusion
  26.2 6.8 %collective-permute-done = bf16[4,512,192]{1,2,0:T(8,128)(2,1)S(1)} collective-permute-done((bf16[4,512,192]{1,2,0:T(8,128)(2,1)}, bf16[4,512,192]{1,2,0:T(8,128)(2,1)S(1)}, u32[]{:S(2)}, u32[]{:S(2)}) %collective-permute-start) | collective-permute-done | bytes 786464 | tf_op jit(solution)/shard_map/ppermute | solution.py:16
  33.1 4.1 %collective-permute-done.1 = bf16[4,512,192]{1,2,0:T(8,128)(2,1)} collective-permute-done((bf16[4,512,192]{1,2,0:T(8,128)(2,1)}, bf16[4,512,192]{1,2,0:T(8,128)(2,1)}, u32[]{:S(2)}, u32[]{:S(2)}) %collective-permute-start.1) | collective-permute-done | bytes 786464 | tf_op jit(solution)/shard_map/ppermute | solution.py:17
  37.2 1.8 pad_maximum_fusion
  39.0 0.0 copy-start.3
  39.0 4.8 %convolution_convert_fusion.1 = bf16[4,8,512,192]{2,1,3,0:T(8,128)(2,1)} fusion(bf16[16,512,192]{1,2,0:T(8,128)(2,1)S(1)} %pad_maximum_fusion, bf16[4,8,16]{2,1,0:T(8,128)(2,1)S(1)} %convert_reduce_fusion), kind=kOutput, calls=%fused_computation.19 | convolution fusion | flops 103809024 | bytes 9438208 | tf_op jit(solution)/shard_map/tij,jlm->tilm/dot_general | solution.py:59
  43.9 58.4 %reduce-scatter.5.cloned.1.call-done = bf16[128,192]{1,0:T(8,128)(2,1)} async-done(((bf16[2048,192]{1,0:T(8,128)(2,1)}), bf16[128,192]{1,0:T(8,128)(2,1)}) %reduce-scatter.5.cloned.1.call-update) | async-done | bytes 49168 | tf_op jit(solution)/shard_map/reduce_scatter | solution.py:66
  102.3 24.9 %all-reduce = bf16[128,192]{1,0:T(8,128)(2,1)S(1)} all-reduce(bf16[128,192]{1,0:T(8,128)(2,1)} %reduce-scatter.5.cloned.1.call-done), channel_id=3, replica_groups=mesh['dom'=8,'blk'=16] {'dom'}, use_global_device_ids=true, to_apply=%region_2.0.clone | all-reduce | flops 24576 | bytes 98304
  127.2 0.3 fusion.52
  127.5 12.9 %all_gather.12 = bf16[128,192]{0,1:T(8,128)(2,1)S(1)} all-gather(bf16[128,24]{0,1:T(8,128)(2,1)S(1)} %fusion.52), channel_id=1, replica_groups=mesh['dom'=8,'blk'=16] {'dom'}, dimensions={1}, use_global_device_ids=true | all-gather | bytes 55296 | tf_op jit(solution)/shard_map/all_gather | solution.py:78
  140.4 24.5 %all_gather.13 = bf16[2048,192]{0,1:T(8,128)(2,1)S(1)} all-gather(bf16[128,192]{0,1:T(8,128)(2,1)S(1)} %all_gather.12), channel_id=1, replica_groups=mesh['dom'=8,'blk'=16] {'blk'}, dimensions={0}, use_global_device_ids=true | all-gather | bytes 835584 | tf_op jit(solution)/shard_map/all_gather | solution.py:83
  164.9 0.2 convert_element_type.81
  165.0 5.2 %fusion.2 = f32[8,192,512]{2,1,0:T(8,128)} fusion(f32[2048,192]{0,1:T(8,128)S(1)} %convert_element_type.81, f32[8,2048]{1,0:T(8,128)S(1)} %get-tuple-element.9, bf16[2048,512]{1,0:T(8,128)(2,1)S(1)} %copy-done), kind=kOutput, calls=%fused_computation.6 | convolution fusion | flops 3227516928 | bytes 6881280 | tf_op jit(solution)/shard_map/gl,pgm->plm/dot_general | solution.py:85
  170.2 13.0 %fusion.42 = bf16[8,512,192]{1,2,0:T(8,128)(2,1)} fusion(bf16[8,512,512]{2,1,0:T(8,128)(2,1)} %param.10, bf16[8,512,192]{1,2,0:T(8,128)(2,1)} %param.9, f32[8,192,512]{2,1,0:T(8,128)} %fusion.2, bf16[4,512,512]{2,1,0:T(8,128)(2,1)} %param.11, bf16[4,8,512,192]{2,1,3,0:T(8,128)(2,1)} %convolution_convert_fusion.1), kind=kOutput, calls=%fused_computation.39 | convolution fusion | flops 4030464000 | bytes 18874368 | tf_op jit(solution)/shard_map/pab,pbm->pam/dot_general | solution.py:51
  183.2 5.3 %fusion = bf16[2048,192]{0,1:T(8,128)(2,1)S(1)} fusion(f32[2048,8]{0,1:T(8,128)S(1)} %get-tuple-element.10, bf16[8,512,192]{1,2,0:T(8,128)(2,1)} %fusion.42, bf16[2048,512]{1,0:T(8,128)(2,1)S(1)} %copy-done), kind=kOutput, calls=%fused_computation.1 | convolution fusion | flops 3227123712 | bytes 4521984 | tf_op jit(solution)/shard_map/gl,plm->pgm/dot_general | solution.py:65
  188.5 1.3 copy.36
  189.8 0.0 reduce-scatter.7.cloned.1.call-update
  189.9 0.0 copy-start.2
  189.9 1.6 fusion.65
  191.5 2.4 collective-permute-start.2
  193.8 1.5 collective-permute-start.3
  195.4 11.6 %collective-permute-done.2 = bf16[4,512,192]{1,2,0:T(8,128)(2,1)S(1)} collective-permute-done((bf16[4,512,192]{1,2,0:T(8,128)(2,1)S(1)}, bf16[4,512,192]{1,2,0:T(8,128)(2,1)S(1)}, u32[]{:S(2)}, u32[]{:S(2)}) %collective-permute-start.2) | collective-permute-done | bytes 786464 | tf_op jit(solution)/shard_map/ppermute | solution.py:16
  207.0 4.5 %collective-permute-done.3 = bf16[4,512,192]{1,2,0:T(8,128)(2,1)S(1)} collective-permute-done((bf16[4,512,192]{1,2,0:T(8,128)(2,1)S(1)}, bf16[4,512,192]{1,2,0:T(8,128)(2,1)S(1)}, u32[]{:S(2)}, u32[]{:S(2)}) %collective-permute-start.3) | collective-permute-done | bytes 786464 | tf_op jit(solution)/shard_map/ppermute | solution.py:17
  211.4 0.4 pad_maximum_fusion.1
  211.8 4.8 %convolution_convert_fusion = bf16[4,8,512,192]{2,1,3,0:T(8,128)(2,1)} fusion(bf16[16,512,192]{1,2,0:T(8,128)(2,1)S(1)} %pad_maximum_fusion.1, bf16[4,8,16]{2,1,0:T(8,128)(2,1)S(1)} %convert_reduce_fusion), kind=kOutput, calls=%fused_computation.18 | convolution fusion | flops 103809024 | bytes 9438208 | tf_op jit(solution)/shard_map/tij,jlm->tilm/dot_general | solution.py:59
  216.7 55.7 %reduce-scatter.7.cloned.1.call-done = bf16[128,192]{1,0:T(8,128)(2,1)} async-done(((bf16[2048,192]{1,0:T(8,128)(2,1)}), bf16[128,192]{1,0:T(8,128)(2,1)}) %reduce-scatter.7.cloned.1.call-update) | async-done | bytes 49168 | tf_op jit(solution)/shard_map/reduce_scatter | solution.py:66
  272.4 24.9 %all-reduce.1 = bf16[128,192]{1,0:T(8,128)(2,1)S(1)} all-reduce(bf16[128,192]{1,0:T(8,128)(2,1)} %reduce-scatter.7.cloned.1.call-done), channel_id=5, replica_groups=mesh['dom'=8,'blk'=16] {'dom'}, use_global_device_ids=true, to_apply=%region_4.0.clone | all-reduce | flops 24576 | bytes 98304
  297.3 0.3 fusion.53
  297.6 12.9 %all_gather.14 = bf16[128,192]{0,1:T(8,128)(2,1)S(1)} all-gather(bf16[128,24]{0,1:T(8,128)(2,1)S(1)} %fusion.53), channel_id=1, replica_groups=mesh['dom'=8,'blk'=16] {'dom'}, dimensions={1}, use_global_device_ids=true | all-gather | bytes 55296 | tf_op jit(solution)/shard_map/all_gather | solution.py:78
  310.4 24.3 %all_gather.15 = bf16[2048,192]{0,1:T(8,128)(2,1)S(1)} all-gather(bf16[128,192]{0,1:T(8,128)(2,1)S(1)} %all_gather.14), channel_id=1, replica_groups=mesh['dom'=8,'blk'=16] {'blk'}, dimensions={0}, use_global_device_ids=true | all-gather | bytes 835584 | tf_op jit(solution)/shard_map/all_gather | solution.py:83
  334.7 0.2 convert_element_type.90
  334.9 5.2 %fusion.3 = f32[8,192,512]{2,1,0:T(8,128)} fusion(f32[2048,192]{0,1:T(8,128)S(1)} %convert_element_type.90, f32[8,2048]{1,0:T(8,128)S(1)} %get-tuple-element.9, bf16[2048,512]{1,0:T(8,128)(2,1)S(1)} %copy-done), kind=kOutput, calls=%fused_computation.7 | convolution fusion | flops 3227516928 | bytes 6881280 | tf_op jit(solution)/shard_map/gl,pgm->plm/dot_general | solution.py:85
  340.1 13.0 %fusion.47 = bf16[8,512,192]{1,2,0:T(8,128)(2,1)} fusion(bf16[8,512,512]{2,1,0:T(8,128)(2,1)} %param.10, bf16[8,512,192]{1,2,0:T(8,128)(2,1)} %param.9, f32[8,192,512]{2,1,0:T(8,128)} %fusion.3, bf16[4,512,512]{2,1,0:T(8,128)(2,1)} %param.11, bf16[4,8,512,192]{2,1,3,0:T(8,128)(2,1)} %convolution_convert_fusion), kind=kOutput, calls=%fused_computation.40 | convolution fusion | flops 4030464000 | bytes 18874368 | tf_op jit(solution)/shard_map/pab,pbm->pam/dot_general | solution.py:51
  (18 shorter events, 0.1 us)
Async XLA Ops:
  6.5 10.8 %copy-start = (bf16[2048,512]{1,0:T(8,128)(2,1)S(1)}, bf16[2048,512]{1,0:T(8,128)(2,1)}, u32[]{:S(2)}) copy-start(bf16[2048,512]{1,0:T(8,128)(2,1)} %param.16) | copy-start | bytes 6291460
  6.5 95.8 %reduce-scatter.5.cloned.1.call-start = ((), (), s32[]{:S(2)}) async-start(), calls=%async_computation.2 | async-start | bytes 1114112 | tf_op jit(solution)/shard_map/reduce_scatter | solution.py:66
  10.9 6.5 %copy-start.1 = (bf16[8,512,192]{1,2,0:T(8,128)(2,1)}, bf16[8,512,192]{1,2,0:T(8,128)(2,1)S(1)}, u32[]{:S(2)}) copy-start(bf16[8,512,192]{1,2,0:T(8,128)(2,1)S(1)} %convolution_convert_fusion.4) | copy-start | bytes 4718596
  10.9 6.4 %copy-start.4 = (bf16[8,2048]{1,0:T(8,128)(2,1)S(1)}, bf16[8,2048]{1,0:T(8,128)(2,1)}, u32[]{:S(2)}) copy-start(bf16[8,2048]{1,0:T(8,128)(2,1)} %param.15) | copy-start | bytes 98308
  12.4 20.7 %collective-permute-start = (bf16[4,512,192]{1,2,0:T(8,128)(2,1)}, bf16[4,512,192]{1,2,0:T(8,128)(2,1)S(1)}, u32[]{:S(2)}, u32[]{:S(2)}) collective-permute-start(bf16[4,512,192]{1,2,0:T(8,128)(2,1)} %get-tuple-element.7), channel_id=1, source_target_pairs={{0,1},{1,2},{2,3},{3,4},{4,5},{5,6},{6,7},{7,8},{8,9},{9,10},{10,1... | collective-permute-start | bytes 2359304 | tf_op jit(solution)/shard_map/ppermute | solution.py:16
  16.0 21.2 %collective-permute-start.1 = (bf16[4,512,192]{1,2,0:T(8,128)(2,1)}, bf16[4,512,192]{1,2,0:T(8,128)(2,1)}, u32[]{:S(2)}, u32[]{:S(2)}) collective-permute-start(bf16[4,512,192]{1,2,0:T(8,128)(2,1)} %get-tuple-element.8), channel_id=1, source_target_pairs={{1,0},{2,1},{3,2},{4,3},{5,4},{6,5},{7,6},{8,7},{9,8},{10,9},{11,1... | collective-permute-start | bytes 2359304 | tf_op jit(solution)/shard_map/ppermute | solution.py:17
  17.4 7.1 %copy-start.5 = (s32[8,6]{1,0:T(8,128)S(1)}, s32[8,6]{1,0:T(8,128)}, u32[]{:S(2)}) copy-start(s32[8,6]{1,0:T(8,128)} %param.12) | copy-start | bytes 580
  17.4 7.2 %copy-start.6 = (s32[8,6]{1,0:T(8,128)S(1)}, s32[8,6]{1,0:T(8,128)}, u32[]{:S(2)}) copy-start(s32[8,6]{1,0:T(8,128)} %param.14) | copy-start | bytes 580
  17.4 7.3 %copy-start.8 = (u32[128]{0:T(128)S(1)}, u32[128]{0:T(128)}, u32[]{:S(2)}) copy-start(u32[128]{0:T(128)} %constant.28) | copy-start | bytes 1540
  17.4 8.6 %copy-start.7 = (s32[8]{0:T(128)S(1)}, s32[8]{0:T(128)}, u32[]{:S(2)}) copy-start(s32[8]{0:T(128)} %param.13) | copy-start | bytes 100
  24.4 247.9 %reduce-scatter.7.cloned.1.call-start = ((), (), s32[]{:S(2)}) async-start(), calls=%async_computation.3 | async-start | bytes 1114112 | tf_op jit(solution)/shard_map/reduce_scatter | solution.py:66
  39.0 88.2 %copy-start.3 = (f32[1,128,128]{2,1,0:T(8,128)S(1)}, f32[1,128,128]{2,1,0:T(8,128)}, u32[]{:S(2)}) copy-start(f32[1,128,128]{2,1,0:T(8,128)} %param.17) | copy-start | bytes 196612
  189.9 21.6 %copy-start.2 = (bf16[8,512,192]{1,2,0:T(8,128)(2,1)S(1)}, bf16[8,512,192]{1,2,0:T(8,128)(2,1)}, u32[]{:S(2)}) copy-start(bf16[8,512,192]{1,2,0:T(8,128)(2,1)} %fusion.42) | copy-start | bytes 4718596
  191.5 15.5 %collective-permute-start.2 = (bf16[4,512,192]{1,2,0:T(8,128)(2,1)S(1)}, bf16[4,512,192]{1,2,0:T(8,128)(2,1)S(1)}, u32[]{:S(2)}, u32[]{:S(2)}) collective-permute-start(bf16[4,512,192]{1,2,0:T(8,128)(2,1)S(1)} %get-tuple-element.5), channel_id=1, source_target_pairs={{0,1},{1,2},{2,3},{3,4},{4,5},{5,6},{6,7},{7,8},{8,9},{9,10},{10,1... | collective-permute-start | bytes 2359304 | tf_op jit(solution)/shard_map/ppermute | solution.py:16
  193.8 17.6 %collective-permute-start.3 = (bf16[4,512,192]{1,2,0:T(8,128)(2,1)S(1)}, bf16[4,512,192]{1,2,0:T(8,128)(2,1)S(1)}, u32[]{:S(2)}, u32[]{:S(2)}) collective-permute-start(bf16[4,512,192]{1,2,0:T(8,128)(2,1)S(1)} %get-tuple-element.6), channel_id=1, source_target_pairs={{1,0},{2,1},{3,2},{4,3},{5,4},{6,5},{7,6},{8,7},{9,8},{10,9},{11,1... | collective-permute-start | bytes 2359304 | tf_op jit(solution)/shard_map/ppermute | solution.py:17
Sparse Core Ops, SparseCore 0:
  24.5 77.7 reduce-scatter.4
  190.0 82.3 reduce-scatter.6
where the time goes:
time: 361 us; the launch traced here: 360 us
  waiting for transfers between devices  141 us (39%)
  blocking collectives  124 us (34%)
  matrix products  61 us (17%)
  between operations  14.4 us (4%)
  starting transfers between devices  8.83 us (2%)
  local copies, waits for them, and re-layouts  7.47 us (2%)
    reduce_scatter x2, waiting for transfers between devices, local(): lax.psum_scatter(jnp.einsum('pg,pgm->gm', phase_wide, spread).astype(jnp....  114 us
    unnamed x2, blocking collectives  49.8 us
    all_gather x2, blocking collectives, local(): lax.all_gather(reflected, 'blk', axis=0, tiled=True).astype(jnp.float32)  48.8 us
    dot_general x3, matrix products, scatter_solve(): jnp.einsum('pab,pbm->pam', t_matrices, source, preferred_element_type=jnp...  30.4 us
    all_gather x2, blocking collectives, local(): lax.all_gather(result.reshape(block_rows, columns).astype(jnp.bfloat16),...  25.7 us
    ppermute x2, waiting for transfers between devices, padded(): before = lax.ppermute(last, axis, up)  18.4 us
    dot_general x2, matrix products, local(): jnp.einsum('gl,pgm->plm', wave_basis, weighted, preferred_element_type=jn...  10.4 us
    dot_general x2, matrix products, local(): jnp.einsum('gl,plm->pgm', wave_basis, current, preferred_element_type=jnp...  10.1 us
  transfers between devices with their start and end apart: 6, of which 6 were waited for; matrix products, arithmetic and copies ran while one was open for 6% of the time, Pallas kernels for 0%

commit v1 on v0

v1 whole, which is shorter than its diff:
```python
import functools

import jax
import jax.numpy as jnp
from jax import lax
from jax.experimental import pallas as pl
from jax.experimental.pallas import tpu as pltpu
from jax.sharding import PartitionSpec as P

ITERS = 2
F32 = jnp.float32
BF16 = jnp.bfloat16
NT_DIMS = (((1,), (1,)), ((), ()))
NN_DIMS = (((1,), (0,)), ((), ()))


def dot(a, b, dims, precision=None):
    return lax.dot_general(a, b, dims, precision=precision, preferred_element_type=F32)


def kernel(
    xs,
    table_ref,
    incident_hbm,
    t_hbm,
    moves_hbm,
    phases_ref,
    basis_hbm,
    grating_ref,
    out_hbm,
    inc_stage,
    out_stage,
    inc_ref,
    t_ref,
    moves_ref,
    basis_ref,
    win,
    halo,
    acc,
    src,
    steps,
    groups,
    pair_out,
    pair_in,
    x_out,
    x_in,
    b_out,
    b_in,
    refl,
    inc_sem,
    t_sem,
    load_sem,
    out_sem,
    pair_s,
    pair_r,
    x_s,
    x_r,
    b_s,
    b_r,
    a_s,
    a_r,
    x2_s,
    x2_r,
    p2_s,
    p2_r,
    halo_s,
    halo_r,
):
    count, _, rows_m = inc_stage.shape
    reach = count // 2
    kinds = moves_ref.shape[0]
    most = (table_ref.shape[1] - kinds) // 2
    width = basis_ref.shape[1]
    total = basis_ref.shape[0]
    half = total // 2
    chunk = half // 2
    order = grating_ref.shape[1]
    doms, blks = 2 * xs, total // order
    per_half = blks // 2
    per_chunk = per_half // 2
    part = rows_m // xs

    dom = lax.axis_index("dom")
    blk = lax.axis_index("blk")
    x, core = dom // 2, dom % 2
    partner = x * 2 + (1 - core)
    linear = dom * blks + blk
    after = lax.rem(linear + 1, doms * blks)
    before = lax.rem(linear + doms * blks - 1, doms * blks)
    after_id = (after // blks, lax.rem(after, blks))
    before_id = (before // blks, lax.rem(before, blks))
    is_owner = blk // per_half == core

    def peer_x(d):
        return lax.rem(x + d, xs) * 2 + core

    def remote(source, target, send, recv, device):
        return pltpu.make_async_remote_copy(
            src_ref=source,
            dst_ref=target,
            send_sem=send,
            recv_sem=recv,
            device_id=device,
            device_id_type=pl.DeviceIdType.MESH,
        )

    def solve_order(i):
        return jnp.where(lax.rem(i, 2) == 0, count - 1 - i // 2, i // 2)

    def inc_load(p):
        return pltpu.make_async_copy(incident_hbm.at[p], inc_stage.at[p], inc_sem.at[p])

    def t_load(p):
        return pltpu.make_async_copy(t_hbm.at[p], t_ref.at[p], t_sem.at[p])

    @pl.loop(0, count)
    def _(i):
        p = solve_order(i)
        inc_load(p).start()
        t_load(p).start()

    basis_load = pltpu.make_async_copy(basis_hbm, basis_ref, load_sem.at[0])
    moves_load = pltpu.make_async_copy(moves_hbm, moves_ref, load_sem.at[1])
    basis_load.start()
    moves_load.start()

    barrier = pltpu.get_barrier_semaphore()

    def greet(device):
        pl.semaphore_signal(
            barrier, inc=1, device_id=device, device_id_type=pl.DeviceIdType.MESH
        )

    greet((partner, blk))
    for d in range(1, xs):
        greet((peer_x(d), blk))

    @pl.loop(1, blks)
    def _(o):
        greet((dom, lax.rem(blk + o, blks)))

    greet(after_id)
    greet(before_id)

    steps[most] = jnp.zeros((rows_m, width), BF16)

    def halo_copy(s, i, to_after):
        if to_after:
            return remote(
                win.at[2 * reach + i], halo.at[s, i], halo_s.at[s, i], halo_r.at[s, i], after_id
            )
        return remote(
            win.at[reach + i],
            halo.at[s, reach + i],
            halo_s.at[s, reach + i],
            halo_r.at[s, reach + i],
            before_id,
        )

    def halo_send(s, batch):
        halo_copy(s, reach - 1 - batch, True).start()
        halo_copy(s, batch, False).start()

    def solve_first(i, carry):
        p = solve_order(i)
        inc_load(p).wait()
        t_load(p).wait()
        turned = inc_stage[p].T
        inc_ref[p] = turned
        win[reach + p] = dot(turned, t_ref[p], NT_DIMS).astype(BF16)
        return carry

    lax.fori_loop(0, reach, solve_first, 0)
    pl.semaphore_wait(barrier, blks - 1 + xs - 1 + 1 + 2)
    for batch in range(reach // 2):
        halo_send(0, batch)
    lax.fori_loop(reach, count, solve_first, 0)

    basis_load.wait()

    def near_field(s, batch):
        lo, hi = reach - 1 - batch, reach + batch
        halo_copy(s, reach - 1 - batch, True).wait_recv()
        halo_copy(s, batch, False).wait_recv()
        win[reach - 1 - batch] = halo[s, reach - 1 - batch]
        win[3 * reach + batch] = halo[s, reach + batch]
        piece = 32 if rows_m % 32 == 0 else rows_m
        for place, p in enumerate((lo, hi)):
            index = [table_ref[p, k] for k in range(most)]
            same = [table_ref[p, most + k].astype(F32) for k in range(most)]
            ends = [table_ref[p, 2 * most + t] for t in range(kinds)]

            @pl.loop(0, rows_m // piece)
            def _(r):
                rows = pl.ds(pl.multiple_of(r * piece, piece), piece)
                run = win[index[0], rows, :].astype(F32)
                steps[0, rows, :] = run.astype(BF16)
                for k in range(1, most):
                    run = run * same[k] + win[index[k], rows, :].astype(F32)
                    steps[k, rows, :] = run.astype(BF16)

            for t in range(kinds):
                groups[t, place * rows_m : (place + 1) * rows_m, :] = steps[ends[t]]
        field = dot(groups[0], moves_ref[0], NT_DIMS)
        for t in range(1, kinds):
            field = field + dot(groups[t], moves_ref[t], NT_DIMS)
        for place, p in enumerate((lo, hi)):
            acc[p] = inc_ref[p].astype(F32) + field[place * rows_m : (place + 1) * rows_m]

    my_rows = pl.ds(pl.multiple_of(x * part, part), part)

    def outward(start):
        cols = pl.ds(pl.multiple_of(start, chunk), chunk)
        spread = dot(
            win[reach : reach + count].reshape(count * rows_m, width), basis_ref[cols, :], NT_DIMS
        ).reshape(count, rows_m, chunk)
        return jnp.sum(spread * phases_ref[:, :, cols].astype(F32), axis=0)

    def inward(s, start, last):
        cols = pl.ds(pl.multiple_of(start, chunk), chunk)
        weighted = (refl[s, :, cols][None] * phases_ref[:, :, cols]).reshape(count * rows_m, chunk)
        back = dot(weighted, basis_ref[cols, :], NN_DIMS).reshape(count, rows_m, width)
        if last:
            src[...] = (acc[...] + back).astype(BF16)
        else:
            acc[...] += back

    def pair_copy(s, j):
        cols = pl.ds(pl.multiple_of(j * chunk, chunk), chunk)
        return remote(
            pair_out.at[s, :, cols],
            pair_in.at[s, :, cols],
            pair_s.at[s, j],
            pair_r.at[s, j],
            (partner, blk),
        )

    def x_copy(s, j, d):
        cols = pl.ds(pl.multiple_of(j * chunk, chunk), chunk)
        their = pl.ds(pl.multiple_of(lax.rem(x + d, xs) * part, part), part)
        return remote(
            x_out.at[s, their, cols],
            x_in.at[s, d - 1, :, cols],
            x_s.at[s, j, d - 1],
            x_r.at[s, j, d - 1],
            (peer_x(d), blk),
        )

    def b_copy(s, b):
        cols = pl.ds(pl.multiple_of(b * order, order), order)
        return remote(
            b_out.at[s, :, cols],
            b_in.at[s, blk],
            b_s.at[s, b],
            b_r.at[s, blk],
            (dom, core * per_half + b),
        )

    def b_arrival(s, sender):
        return remote(
            b_out.at[s, :, pl.ds(0, order)],
            b_in.at[s, sender],
            b_s.at[s, 0],
            b_r.at[s, sender],
            (dom, sender),
        )

    def refl_at(s, b):
        cols = pl.ds(pl.multiple_of((core * per_half + b) * order, order), order)
        return refl.at[s, my_rows, cols]

    mine = lax.rem(blk, per_half)

    def a_copy(s, o):
        return remote(
            refl_at(s, mine),
            refl_at(s, mine),
            a_s.at[s, o],
            a_r.at[s, mine],
            (dom, lax.rem(blk + o, blks)),
        )

    def a_arrival(s, b):
        return remote(
            refl_at(s, b), refl_at(s, b), a_s.at[s, 0], a_r.at[s, b], (dom, core * per_half + b)
        )

    def x2_copy(s, d, b):
        return remote(
            refl_at(s, b),
            refl_at(s, b),
            x2_s.at[s, d - 1, b],
            x2_r.at[s, d - 1, b],
            (peer_x(d), blk),
        )

    def x2_arrival(s, d, b):
        theirs = pl.ds(pl.multiple_of(lax.rem(x + xs - d, xs) * part, part), part)
        cols = pl.ds(pl.multiple_of((core * per_half + b) * order, order), order)
        place = refl.at[s, theirs, cols]
        return remote(
            place, place, x2_s.at[s, d - 1, b], x2_r.at[s, d - 1, b], (peer_x(xs - d), blk)
        )

    def p2_copy(s, j, sender):
        cols = pl.ds(pl.multiple_of(sender * half + j * chunk, chunk), chunk)
        return remote(
            refl.at[s, :, cols], refl.at[s, :, cols], p2_s.at[s, j], p2_r.at[s, j], (partner, blk)
        )

    @pl.loop(0, ITERS)
    def _(s):
        @pl.loop(0, 2)
        def _(j):
            cols = pl.ds(pl.multiple_of(j * chunk, chunk), chunk)
            pair_out[s, :, cols] = outward((1 - core) * half + j * chunk).astype(BF16)
            pair_copy(s, j).start()

        @pl.loop(0, 2)
        def _(j):
            cols = pl.ds(pl.multiple_of(j * chunk, chunk), chunk)
            own = outward(core * half + j * chunk)
            pair_copy(s, j).wait_recv()
            x_out[s, :, cols] = (own + pair_in[s, :, cols].astype(F32)).astype(BF16)
            for d in range(1, xs):
                x_copy(s, j, d).start()

        @pl.when(s == 0)
        def _():
            moves_load.wait()

        near_field(s, 0)

        @pl.loop(0, 2)
        def _(j):
            cols = pl.ds(pl.multiple_of(j * chunk, chunk), chunk)
            both = x_out[s, my_rows, cols].astype(F32)
            for d in range(1, xs):
                x_copy(s, j, d).wait_recv()
                both = both + x_in[s, d - 1, :, cols].astype(F32)
            b_out[s, :, cols] = both.astype(BF16)

            @pl.loop(0, per_chunk)
            def _(i):
                b = j * per_chunk + i

                @pl.when(core * per_half + b != blk)
                def _():
                    b_copy(s, b).start()

        halo_send(s, 2)
        near_field(s, 1)

        @pl.when(is_owner)
        def _():
            own_cols = pl.ds(pl.multiple_of(mine * order, order), order)

            def gather(o, so_far):
                sender = lax.rem(blk + o, blks)
                b_arrival(s, sender).wait_recv()
                return so_far + b_in[s, sender].astype(F32)

            sums = lax.fori_loop(1, blks, gather, b_out[s, :, own_cols].astype(F32))
            result = dot(sums, grating_ref[0], NT_DIMS, lax.Precision.HIGHEST)
            out_cols = pl.ds(pl.multiple_of(blk * order, order), order)
            refl[s, my_rows, out_cols] = result.astype(BF16)

            @pl.loop(1, blks)
            def _(o):
                a_copy(s, o).start()

        halo_send(s, 3)
        near_field(s, 2)

        @pl.loop(0, per_half)
        def _(o):
            b = lax.rem(mine + o, per_half)

            @pl.when(core * per_half + b != blk)
            def _():
                a_arrival(s, b).wait_recv()

            for d in range(1, xs):
                x2_copy(s, d, b).start()

        near_field(s, 3)

        for j in range(2):

            @pl.loop(0, per_chunk)
            def _(i):
                b = j * per_chunk + i
                for d in range(1, xs):
                    x2_arrival(s, d, b).wait_recv()

            p2_copy(s, j, core).start()
        for j in range(2):
            inward(s, core * half + j * chunk, False)
        for j in range(2):
            p2_copy(s, j, 1 - core).wait_recv()
            inward(s, (1 - core) * half + j * chunk, j == 1)

        for i in range(reach):
            halo_copy(s, i, True).wait_send()
            halo_copy(s, i, False).wait_send()
        for j in range(2):
            pair_copy(s, j).wait_send()
            p2_copy(s, j, core).wait_send()
            for d in range(1, xs):
                x_copy(s, j, d).wait_send()

        @pl.loop(0, per_half)
        def _(b):
            for d in range(1, xs):
                x2_copy(s, d, b).wait_send()

            @pl.when(core * per_half + b != blk)
            def _():
                b_copy(s, b).wait_send()

        @pl.when(is_owner)
        def _():
            @pl.loop(1, blks)
            def _(o):
                a_copy(s, o).wait_send()

        @pl.when(s < ITERS - 1)
        def _():
            def solve_next(i, carry):
                p = solve_order(i)
                win[reach + p] = dot(src[p], t_ref[p], NT_DIMS).astype(BF16)
                return carry

            lax.fori_loop(0, reach, solve_next, 0)
            for batch in range(reach // 2):
                halo_send(s + 1, batch)
            lax.fori_loop(reach, count, solve_next, 0)

    def out_copy(p):
        return pltpu.make_async_copy(out_stage.at[p], out_hbm.at[p], out_sem.at[p])

    @pl.loop(0, count)
    def _(p):
        out_stage[p] = dot(t_ref[p], src[p], NT_DIMS).astype(BF16)
        out_copy(p).start()

    @pl.loop(0, count)
    def _(p):
        out_copy(p).wait()


def slot_table(near_index, near_count, near_type, first, kinds, reach):
    most = near_index.shape[1]
    place = jnp.arange(most)
    slots = near_index - first + reach
    key = jnp.where(place[None, :] < near_count[:, None], near_type, kinds)
    ahead = (key[:, :, None] < key[:, None, :]) | (
        (key[:, :, None] == key[:, None, :]) & (place[:, None] < place[None, :])[None]
    )
    rank = jnp.sum(ahead.astype(jnp.int32), axis=1)
    hit = (rank[:, :, None] == place[None, None, :]).astype(jnp.int32)
    index = jnp.sum(hit * slots[:, :, None], axis=1)
    key_sorted = jnp.sum(hit * key[:, :, None], axis=1)
    same = jnp.concatenate(
        [jnp.zeros_like(key[:, :1]), (key_sorted[:, 1:] == key_sorted[:, :-1]).astype(jnp.int32)],
        axis=1,
    )
    kind = jnp.arange(kinds)[None, None, :]
    upto = jnp.sum((key[:, :, None] <= kind).astype(jnp.int32), axis=1)
    some = jnp.any(key[:, :, None] == kind, axis=1)
    ends = jnp.where(some, upto - 1, most)
    return jnp.concatenate([index, same, ends], axis=1).astype(jnp.int32)


def local(
    incident,
    t_matrices,
    translations,
    near_index,
    near_count,
    near_type,
    phases,
    wave_basis,
    grating_blocks,
):
    doms, blks = lax.axis_size("dom"), lax.axis_size("blk")
    xs = doms // 2
    count, width, rows_m = incident.shape
    reach = count // 2
    kinds = translations.shape[0]
    most = near_index.shape[1]
    total = wave_basis.shape[0]
    half = total // 2
    order = grating_blocks.shape[1]
    part = rows_m // xs
    per_half = blks // 2
    first = lax.axis_index(("dom", "blk")) * count
    table = slot_table(near_index, near_count, near_type, first, kinds, reach)
    hbm = pl.BlockSpec(memory_space=pl.ANY)
    vmem = pl.BlockSpec(memory_space=pltpu.VMEM)
    sem = pltpu.SemaphoreType.DMA
    n = ITERS
    return pl.pallas_call(
        functools.partial(kernel, xs),
        out_shape=jax.ShapeDtypeStruct(incident.shape, BF16),
        in_specs=[pl.BlockSpec(memory_space=pltpu.SMEM), hbm, hbm, hbm, vmem, hbm, vmem],
        out_specs=hbm,
        scratch_shapes=[
            pltpu.VMEM((count, width, rows_m), BF16),
            pltpu.VMEM((count, width, rows_m), BF16),
            pltpu.VMEM((count, rows_m, width), BF16),
            pltpu.VMEM((count, width, width), BF16),
            pltpu.VMEM((kinds, width, width), BF16),
            pltpu.VMEM((total, width), BF16),
            pltpu.VMEM((count + 2 * reach, rows_m, width), BF16),
            pltpu.VMEM((n, 2 * reach, rows_m, width), BF16),
            pltpu.VMEM((count, rows_m, width), F32),
            pltpu.VMEM((count, rows_m, width), BF16),
            pltpu.VMEM((most + 1, rows_m, width), BF16),
            pltpu.VMEM((kinds, 2 * rows_m, width), BF16),
            pltpu.VMEM((n, rows_m, half), BF16),
            pltpu.VMEM((n, rows_m, half), BF16),
            pltpu.VMEM((n, rows_m, half), BF16),
            pltpu.VMEM((n, xs - 1, part, half), BF16),
            pltpu.VMEM((n, part, half), BF16),
            pltpu.VMEM((n, blks, part, order), BF16),
            pltpu.VMEM((n, rows_m, total), BF16),
            sem((count,)),
            sem((count,)),
            sem((2,)),
            sem((count,)),
            sem((n, 2)),
            sem((n, 2)),
            sem((n, 2, xs - 1)),
            sem((n, 2, xs - 1)),
            sem((n, per_half)),
            sem((n, blks)),
            sem((n, blks)),
            sem((n, per_half)),
            sem((n, xs - 1, per_half)),
            sem((n, xs - 1, per_half)),
            sem((n, 2)),
            sem((n, 2)),
            sem((n, 2 * reach)),
            sem((n, 2 * reach)),
        ],
        compiler_params=pltpu.CompilerParams(
            collective_id=0, has_side_effects=True, vmem_limit_bytes=60 * 2**20
        ),
    )(
        table,
        incident,
        t_matrices,
        translations,
        phases.reshape(count, 1, total),
        wave_basis,
        grating_blocks,
    )


def solution(mesh):
    placed = (
        P(("dom", "blk"), None, None),
        P(("dom", "blk"), None, None),
        P(),
        P(("dom", "blk"), None),
        P(("dom", "blk")),
        P(("dom", "blk"), None),
        P(("dom", "blk"), None),
        P(),
        P("blk", None, None),
    )
    return jax.shard_map(
        local, mesh=mesh, in_specs=placed, out_specs=P(("dom", "blk"), None, None), check_vma=False
    )
```

time: 361 us -> 96 us (0.27)
  waiting for transfers between devices: 141 us -> 0 us
  blocking collectives: 124 us -> 0 us
  Pallas kernels: 0 us -> 83.6 us
  matrix products: 61 us -> 0 us
  between operations: 14.4 us -> 0.03 us
  starting transfers between devices: 8.83 us -> 0 us
    reduce_scatter x2 -> x0, waiting for transfers between devices: 114 us -> none  [local(): lax.psum_scatter(jnp.einsum('pg,pgm->gm', phase_wide, spread).astype(jnp....]
    pallas_call x0 -> x1, Pallas kernels: none -> 83.6 us  [local(): pl.pallas_call(functools.partial(kernel, xs), out_shape=jax.ShapeDtypeStr...]
    all_gather x4 -> x0, blocking collectives: 74.5 us -> none  [the longest x2 48.8 us: local(): lax.all_gather(reflected, 'blk', axis=0, tiled=True).astype(jnp.float32)]
    dot_general x11 -> x0, matrix products: 61 us -> none  [the longest x3 30.4 us: scatter_solve(): jnp.einsum('pab,pbm->pam', t_matrices, source, preferred_element_type=jnp...]
    unnamed x2 -> x0, blocking collectives: 49.8 us -> none
    ppermute x4 -> x0, waiting for transfers between devices: 27 us -> none  [the longest x2 18.4 us: padded(): before = lax.ppermute(last, axis, up)]
    ppermute x4 -> x0, starting transfers between devices: 8.79 us -> none  [the longest x2 5.98 us: padded(): before = lax.ppermute(last, axis, up)]
    pallas_call x0 -> x1, local copies, waits for them, and re-layouts: none -> 3.85 us  [local(): pl.pallas_call(functools.partial(kernel, xs), out_shape=jax.ShapeDtypeStr...]
  transfers between devices with their start and end apart: 6 -> 0, of which waited for: 6 -> 0; matrix products, arithmetic and copies ran while one was open for 6% -> 0% of each run, Pallas kernels for 0% -> 0%
where the time goes in v1:
time: 96 us; the launch traced here: 95.6 us
  Pallas kernels  83.6 us (87%)
  local copies, waits for them, and re-layouts  9.5 us (10%)
  other arithmetic  2.42 us (3%)
    pallas_call x1, Pallas kernels, local(): pl.pallas_call(functools.partial(kernel, xs), out_shape=jax.ShapeDtypeStr...  83.6 us
    pallas_call x1, local copies, waits for them, and re-layouts, local(): pl.pallas_call(functools.partial(kernel, xs), out_shape=jax.ShapeDtypeStr...  3.85 us
    unnamed x1, local copies, waits for them, and re-layouts  3.71 us

profile of v1, /device:TPU:0, one launch (start us, length us, event | category | flops | bytes accessed | tf_op | source)
XLA Modules:
  0.0 95.6 jit_solution(3767514442547580861)
XLA Ops:
  0.0 0.1 pad.1.clone
  0.1 0.7 subtract_add_fusion
  0.8 0.1 copy.17
  0.9 0.8 fusion.1
  1.6 0.1 copy.15
  1.7 0.1 convert_reduce_fusion
  1.8 0.1 copy.16
  1.9 0.1 select_reduce_fusion.1
  2.0 0.1 copy.20
  2.1 0.1 copy.19
  2.2 0.1 fusion.2
  2.3 0.7 pad_add_fusion.table_ref
  2.9 1.4 %copy.22.phases_ref = bf16[8,1,2048]{2,1,0:T(2,128)(2,1)} copy(bf16[8,1,2048]{2,0,1:T(8,128)(2,1)} %bitcast.2) | data formatting | bytes 65536 | tf_op jit(solution)/shard_map/reshape | solution.py:555
  4.4 3.7 %copy.21.incident_hbm = bf16[8,512,192]{2,1,0:T(8,128)(2,1)} copy(bf16[8,512,192]{1,2,0:T(8,128)(2,1)} %param.9) | data formatting | bytes 3145728 | tf_op args[0]
  8.1 83.6 %shard_map.91 = bf16[8,512,192]{2,1,0:T(8,128)(2,1)} custom-call(s32[8,16]{1,0:T(8,128)} %pad_add_fusion.table_ref, bf16[8,512,192]{2,1,0:T(8,128)(2,1)} %copy.21.incident_hbm, bf16[8,512,512]{2,1,0:T(8,128)(2,1)} %t_hbm.1, bf16[4,512,512]{2,1,0:T(8,128)(2,1)} %moves_hbm.1, bf16[8,1,2048]{2,1,0:T(2,128)(2,1)} %copy.22.phases_ref, ...), custom_call_target="tpu_custom_call" | custom-call | tf_op jit(solution)/shard_map/pallas_call | solution.py:503
  91.7 3.9 %copy.23 = bf16[8,512,192]{1,2,0:T(8,128)(2,1)} copy(bf16[8,512,192]{2,1,0:T(8,128)(2,1)} %shard_map.91) | data formatting | bytes 3145728 | tf_op jit(solution)/shard_map/pallas_call | solution.py:503
  (4 shorter events, 0.0 us)

commit v2 on v1

--- a/solution.py
+++ b/solution.py
@@ -20,17 +20,22 @@
 
 def kernel(
     xs,
-    table_ref,
+    index_ref,
+    count_ref,
+    type_ref,
     incident_hbm,
     t_hbm,
     moves_hbm,
+    phases_hbm,
+    basis_hbm,
+    grating_hbm,
+    out_hbm,
+    table_ref,
+    phases_flat,
     phases_ref,
-    basis_hbm,
     grating_ref,
-    out_hbm,
-    inc_stage,
+    inc_ref,
     out_stage,
-    inc_ref,
     t_ref,
     moves_ref,
     basis_ref,
@@ -66,10 +71,10 @@
     halo_s,
     halo_r,
 ):
-    count, _, rows_m = inc_stage.shape
+    count, rows_m, _ = inc_ref.shape
     reach = count // 2
     kinds = moves_ref.shape[0]
-    most = (table_ref.shape[1] - kinds) // 2
+    most = index_ref.shape[1]
     width = basis_ref.shape[1]
     total = basis_ref.shape[0]
     half = total // 2
@@ -108,7 +113,7 @@
         return jnp.where(lax.rem(i, 2) == 0, count - 1 - i // 2, i // 2)
 
     def inc_load(p):
-        return pltpu.make_async_copy(incident_hbm.at[p], inc_stage.at[p], inc_sem.at[p])
+        return pltpu.make_async_copy(incident_hbm.at[p], inc_ref.at[p], inc_sem.at[p])
 
     def t_load(p):
         return pltpu.make_async_copy(t_hbm.at[p], t_ref.at[p], t_sem.at[p])
@@ -121,6 +126,10 @@
 
     basis_load = pltpu.make_async_copy(basis_hbm, basis_ref, load_sem.at[0])
     moves_load = pltpu.make_async_copy(moves_hbm, moves_ref, load_sem.at[1])
+    phases_load = pltpu.make_async_copy(phases_hbm, phases_flat, load_sem.at[2])
+    grating_load = pltpu.make_async_copy(grating_hbm, grating_ref, load_sem.at[3])
+    phases_load.start()
+    grating_load.start()
     basis_load.start()
     moves_load.start()
 
@@ -143,6 +152,39 @@
     greet(before_id)
 
     steps[most] = jnp.zeros((rows_m, width), BF16)
+
+    @pl.loop(0, count)
+    def _(p):
+        live = count_ref[p]
+        slot = [
+            jnp.clip(index_ref[p, k] - linear * count + reach, 0, count + 2 * reach - 1)
+            for k in range(most)
+        ]
+        key = [jnp.where(k < live, type_ref[p, k], kinds) for k in range(most)]
+        rank = [jnp.int32(0)] * most
+        for k in range(most):
+            for n in range(k + 1, most):
+                later = (key[n] < key[k]).astype(jnp.int32)
+                rank[k] = rank[k] + later
+                rank[n] = rank[n] + (1 - later)
+        sorted_slot, sorted_key = [], []
+        for r in range(most):
+            here, kind = slot[0], key[0]
+            for k in range(1, most):
+                hit = rank[k] == r
+                here = jnp.where(hit, slot[k], here)
+                kind = jnp.where(hit, key[k], kind)
+            sorted_slot.append(here)
+            sorted_key.append(kind)
+        for r in range(most):
+            table_ref[p, r] = sorted_slot[r]
+            if r > 0:
+                table_ref[p, most + r] = (sorted_key[r] == sorted_key[r - 1]).astype(jnp.int32)
+        for t in range(kinds):
+            last = jnp.int32(most)
+            for r in range(most):
+                last = jnp.where(sorted_key[r] == t, r, last)
+            table_ref[p, 2 * most + t] = last
 
     def halo_copy(s, i, to_after):
         if to_after:
@@ -165,9 +207,7 @@
         p = solve_order(i)
         inc_load(p).wait()
         t_load(p).wait()
-        turned = inc_stage[p].T
-        inc_ref[p] = turned
-        win[reach + p] = dot(turned, t_ref[p], NT_DIMS).astype(BF16)
+        win[reach + p] = dot(inc_ref[p], t_ref[p], NT_DIMS).astype(BF16)
         return carry
 
     lax.fori_loop(0, reach, solve_first, 0)
@@ -176,6 +216,9 @@
         halo_send(0, batch)
     lax.fori_loop(reach, count, solve_first, 0)
 
+    phases_load.wait()
+    for p in range(count):
+        phases_ref[p] = phases_flat[p : p + 1, :]
     basis_load.wait()
 
     def near_field(s, batch):
@@ -187,7 +230,7 @@
         piece = 32 if rows_m % 32 == 0 else rows_m
         for place, p in enumerate((lo, hi)):
             index = [table_ref[p, k] for k in range(most)]
-            same = [table_ref[p, most + k].astype(F32) for k in range(most)]
+            same = [table_ref[p, most + k].astype(F32) if k else None for k in range(most)]
             ends = [table_ref[p, 2 * most + t] for t in range(kinds)]
 
             @pl.loop(0, rows_m // piece)
@@ -328,6 +371,7 @@
         @pl.when(s == 0)
         def _():
             moves_load.wait()
+            grating_load.wait()
 
         near_field(s, 0)
 
@@ -441,35 +485,12 @@
 
     @pl.loop(0, count)
     def _(p):
-        out_stage[p] = dot(t_ref[p], src[p], NT_DIMS).astype(BF16)
+        out_stage[p] = dot(src[p], t_ref[p], NT_DIMS).astype(BF16)
         out_copy(p).start()
 
     @pl.loop(0, count)
     def _(p):
         out_copy(p).wait()
-
-
-def slot_table(near_index, near_count, near_type, first, kinds, reach):
-    most = near_index.shape[1]
-    place = jnp.arange(most)
-    slots = near_index - first + reach
-    key = jnp.where(place[None, :] < near_count[:, None], near_type, kinds)
-    ahead = (key[:, :, None] < key[:, None, :]) | (
-        (key[:, :, None] == key[:, None, :]) & (place[:, None] < place[None, :])[None]
-    )
-    rank = jnp.sum(ahead.astype(jnp.int32), axis=1)
-    hit = (rank[:, :, None] == place[None, None, :]).astype(jnp.int32)
-    index = jnp.sum(hit * slots[:, :, None], axis=1)
-    key_sorted = jnp.sum(hit * key[:, :, None], axis=1)
-    same = jnp.concatenate(
-        [jnp.zeros_like(key[:, :1]), (key_sorted[:, 1:] == key_sorted[:, :-1]).astype(jnp.int32)],
-        axis=1,
-    )
-    kind = jnp.arange(kinds)[None, None, :]
-    upto = jnp.sum((key[:, :, None] <= kind).astype(jnp.int32), axis=1)
-    some = jnp.any(key[:, :, None] == kind, axis=1)
-    ends = jnp.where(some, upto - 1, most)
-    return jnp.concatenate([index, same, ends], axis=1).astype(jnp.int32)
 
 
 def local(
@@ -486,6 +507,7 @@
     doms, blks = lax.axis_size("dom"), lax.axis_size("blk")
     xs = doms // 2
     count, width, rows_m = incident.shape
+    turned = (count, rows_m, width)
     reach = count // 2
     kinds = translations.shape[0]
     most = near_index.shape[1]
@@ -494,21 +516,22 @@
     order = grating_blocks.shape[1]
     part = rows_m // xs
     per_half = blks // 2
-    first = lax.axis_index(("dom", "blk")) * count
-    table = slot_table(near_index, near_count, near_type, first, kinds, reach)
     hbm = pl.BlockSpec(memory_space=pl.ANY)
-    vmem = pl.BlockSpec(memory_space=pltpu.VMEM)
+    smem = pl.BlockSpec(memory_space=pltpu.SMEM)
     sem = pltpu.SemaphoreType.DMA
     n = ITERS
-    return pl.pallas_call(
+    result = pl.pallas_call(
         functools.partial(kernel, xs),
-        out_shape=jax.ShapeDtypeStruct(incident.shape, BF16),
-        in_specs=[pl.BlockSpec(memory_space=pltpu.SMEM), hbm, hbm, hbm, vmem, hbm, vmem],
+        out_shape=jax.ShapeDtypeStruct(turned, BF16),
+        in_specs=[smem] * 3 + [hbm] * 6,
         out_specs=hbm,
         scratch_shapes=[
-            pltpu.VMEM((count, width, rows_m), BF16),
-            pltpu.VMEM((count, width, rows_m), BF16),
-            pltpu.VMEM((count, rows_m, width), BF16),
+            pltpu.SMEM((count, 2 * most + kinds), jnp.int32),
+            pltpu.VMEM((count, total), BF16),
+            pltpu.VMEM((count, 1, total), BF16),
+            pltpu.VMEM((1, order, order), F32),
+            pltpu.VMEM(turned, BF16),
+            pltpu.VMEM(turned, BF16),
             pltpu.VMEM((count, width, width), BF16),
             pltpu.VMEM((kinds, width, width), BF16),
             pltpu.VMEM((total, width), BF16),
@@ -527,7 +550,7 @@
             pltpu.VMEM((n, rows_m, total), BF16),
             sem((count,)),
             sem((count,)),
-            sem((2,)),
+            sem((4,)),
             sem((count,)),
             sem((n, 2)),
             sem((n, 2)),
@@ -548,14 +571,17 @@
             collective_id=0, has_side_effects=True, vmem_limit_bytes=60 * 2**20
         ),
     )(
-        table,
-        incident,
+        near_index,
+        near_count,
+        near_type,
+        jnp.swapaxes(incident, 1, 2),
         t_matrices,
         translations,
-        phases.reshape(count, 1, total),
+        phases,
         wave_basis,
         grating_blocks,
     )
+    return jnp.swapaxes(result, 1, 2)
 
 
 def solution(mesh):

time: 96 us -> 85.4 us (0.89)
  local copies, waits for them, and re-layouts: 9.5 us -> 2.65 us
  other arithmetic: 2.42 us -> 0 us
  Pallas kernels: 83.6 us -> 82.6 us
    pallas_call x1 -> x0, local copies, waits for them, and re-layouts: 3.85 us -> none  [local(): pl.pallas_call(functools.partial(kernel, xs), out_shape=jax.ShapeDtypeStr...]
    reshape x1 -> x0, local copies, waits for them, and re-layouts: 1.44 us -> none  [local(): phases.reshape(count, 1, total)]
    unnamed x1, local copies, waits for them, and re-layouts: 3.71 us -> 2.65 us
    pallas_call x1, Pallas kernels: 83.6 us -> 82.6 us  [local(): pl.pallas_call(functools.partial(kernel, xs), out_shape=jax.ShapeDtypeStr...]
where the time goes in v2:
time: 85.4 us; the launch traced here: 85.2 us
  Pallas kernels  82.6 us (97%)
  local copies, waits for them, and re-layouts  2.65 us (3%)
    pallas_call x1, Pallas kernels, local(): pl.pallas_call(functools.partial(kernel, xs), out_shape=jax.ShapeDtypeStr...  82.6 us
    unnamed x1, local copies, waits for them, and re-layouts  2.65 us

profile of v2, /device:TPU:0, one launch (start us, length us, event | category | flops | bytes accessed | tf_op | source)
XLA Modules:
  0.0 85.2 jit_solution(15713442527219810704)
XLA Ops:
  0.0 82.6 %shard_map.91 = bf16[8,192,512]{2,1,0:T(8,128)(2,1)} custom-call(s32[8,6]{1,0:T(8,128)} %index_ref.1, s32[8]{0:T(128)} %count_ref.1, s32[8,6]{1,0:T(8,128)} %type_ref.1, bf16[8,192,512]{2,1,0:T(8,128)(2,1)} %bitcast.3, bf16[8,512,512]{2,1,0:T(8,128)(2,1)} %t_hbm.1, bf16[4,512,512]{2,1,0:T(8,128)(2,1)} %moves_hbm.1, bf16[8,2048]{1,0:T(8,128)(2,1)} %phases_hbm.1, ...), custom_call_target="tpu_custom_call" | custom-call | tf_op jit(solution)/shard_map/pallas_call | solution.py:523
  82.6 2.7 %copy.11 = bf16[8,512,192]{1,2,0:T(8,128)(2,1)} copy(bf16[8,512,192]{1,2,0:T(8,128)(2,1)} %bitcast.2) | data formatting | bytes 3145728

commit v3 on v2

--- a/solution.py
+++ b/solution.py
@@ -20,6 +20,7 @@
 
 def kernel(
     xs,
+    zs,
     index_ref,
     count_ref,
     type_ref,
@@ -35,7 +36,6 @@
     phases_ref,
     grating_ref,
     inc_ref,
-    out_stage,
     t_ref,
     moves_ref,
     basis_ref,
@@ -55,6 +55,7 @@
     inc_sem,
     t_sem,
     load_sem,
+    basis_sem,
     out_sem,
     pair_s,
     pair_r,
@@ -81,23 +82,30 @@
     chunk = half // 2
     order = grating_ref.shape[1]
     doms, blks = 2 * xs, total // order
-    per_half = blks // 2
-    per_chunk = per_half // 2
+    ys = blks // zs
     part = rows_m // xs
 
     dom = lax.axis_index("dom")
     blk = lax.axis_index("blk")
-    x, core = dom // 2, dom % 2
+    x, core = dom // 2, lax.rem(dom, 2)
+    z, y = blk // ys, lax.rem(blk, ys)
     partner = x * 2 + (1 - core)
     linear = dom * blks + blk
     after = lax.rem(linear + 1, doms * blks)
     before = lax.rem(linear + doms * blks - 1, doms * blks)
     after_id = (after // blks, lax.rem(after, blks))
     before_id = (before // blks, lax.rem(before, blks))
-    is_owner = blk // per_half == core
+
+    is_owner = y // 2 == core
+
+    def at_x(d):
+        return lax.rem(x + d, xs)
+
+    def at_z(d):
+        return lax.rem(z + d, zs)
 
     def peer_x(d):
-        return lax.rem(x + d, xs) * 2 + core
+        return (at_x(d) * 2 + core, blk)
 
     def remote(source, target, send, recv, device):
         return pltpu.make_async_remote_copy(
@@ -124,13 +132,24 @@
         inc_load(p).start()
         t_load(p).start()
 
-    basis_load = pltpu.make_async_copy(basis_hbm, basis_ref, load_sem.at[0])
+    def basis_load(q):
+        b = lax.rem(q, zs) * ys + q // zs
+        return pltpu.make_async_copy(
+            basis_hbm.at[pl.ds(pl.multiple_of(b * order, order), order), :],
+            basis_ref.at[pl.ds(pl.multiple_of(q * order, order), order), :],
+            basis_sem.at[q],
+        )
+
     moves_load = pltpu.make_async_copy(moves_hbm, moves_ref, load_sem.at[1])
     phases_load = pltpu.make_async_copy(phases_hbm, phases_flat, load_sem.at[2])
     grating_load = pltpu.make_async_copy(grating_hbm, grating_ref, load_sem.at[3])
     phases_load.start()
     grating_load.start()
-    basis_load.start()
+
+    @pl.loop(0, blks)
+    def _(q):
+        basis_load(q).start()
+
     moves_load.start()
 
     barrier = pltpu.get_barrier_semaphore()
@@ -141,8 +160,9 @@
         )
 
     greet((partner, blk))
+
     for d in range(1, xs):
-        greet((peer_x(d), blk))
+        greet(peer_x(d))
 
     @pl.loop(1, blks)
     def _(o):
@@ -211,21 +231,26 @@
         return carry
 
     lax.fori_loop(0, reach, solve_first, 0)
-    pl.semaphore_wait(barrier, blks - 1 + xs - 1 + 1 + 2)
-    for batch in range(reach // 2):
-        halo_send(0, batch)
+    pl.semaphore_wait(barrier, 1 + (blks - 1) + (xs - 1) + 2)
+    halo_send(0, 0)
     lax.fori_loop(reach, count, solve_first, 0)
-
     phases_load.wait()
     for p in range(count):
-        phases_ref[p] = phases_flat[p : p + 1, :]
-    basis_load.wait()
+        for q in range(blks):
+            b = (q % zs) * ys + q // zs
+            phases_ref[p, :, q * order : (q + 1) * order] = phases_flat[
+                p : p + 1, b * order : (b + 1) * order
+            ]
+
+    @pl.loop(0, blks)
+    def _(q):
+        basis_load(q).wait()
 
     def near_field(s, batch):
         lo, hi = reach - 1 - batch, reach + batch
         halo_copy(s, reach - 1 - batch, True).wait_recv()
         halo_copy(s, batch, False).wait_recv()
-        win[reach - 1 - batch] = halo[s, reach - 1 - batch]
+        win[lo] = halo[s, lo]
         win[3 * reach + batch] = halo[s, reach + batch]
         piece = 32 if rows_m % 32 == 0 else rows_m
         for place, p in enumerate((lo, hi)):
@@ -259,155 +284,136 @@
         ).reshape(count, rows_m, chunk)
         return jnp.sum(spread * phases_ref[:, :, cols].astype(F32), axis=0)
 
-    def inward(s, start, last):
-        cols = pl.ds(pl.multiple_of(start, chunk), chunk)
-        weighted = (refl[s, :, cols][None] * phases_ref[:, :, cols]).reshape(count * rows_m, chunk)
-        back = dot(weighted, basis_ref[cols, :], NN_DIMS).reshape(count, rows_m, width)
+    def inward(s, rows, start, last):
+        cols = pl.ds(pl.multiple_of(start, half), half)
+        weighted = (refl[s, rows, cols][None] * phases_ref[:, :, cols]).reshape(count * part, half)
+        back = dot(weighted, basis_ref[cols, :], NN_DIMS).reshape(count, part, width)
         if last:
-            src[...] = (acc[...] + back).astype(BF16)
+            src[:, rows, :] = (acc[:, rows, :] + back).astype(BF16)
         else:
-            acc[...] += back
+            acc[:, rows, :] += back
+
+    def columns(start, size):
+        return pl.ds(pl.multiple_of(start, order), size)
+
+    def x_rows(i):
+        return pl.ds(pl.multiple_of(i * part, part), part)
+
+    def chunk_cols(j):
+        return columns(j * chunk, chunk)
 
     def pair_copy(s, j):
-        cols = pl.ds(pl.multiple_of(j * chunk, chunk), chunk)
         return remote(
-            pair_out.at[s, :, cols],
-            pair_in.at[s, :, cols],
+            pair_out.at[s, :, chunk_cols(j)],
+            pair_in.at[s, :, chunk_cols(j)],
             pair_s.at[s, j],
             pair_r.at[s, j],
             (partner, blk),
         )
 
     def x_copy(s, j, d):
-        cols = pl.ds(pl.multiple_of(j * chunk, chunk), chunk)
-        their = pl.ds(pl.multiple_of(lax.rem(x + d, xs) * part, part), part)
         return remote(
-            x_out.at[s, their, cols],
-            x_in.at[s, d - 1, :, cols],
+            x_out.at[s, x_rows(at_x(d)), chunk_cols(j)],
+            x_in.at[s, d - 1, :, chunk_cols(j)],
             x_s.at[s, j, d - 1],
             x_r.at[s, j, d - 1],
-            (peer_x(d), blk),
-        )
-
-    def b_copy(s, b):
-        cols = pl.ds(pl.multiple_of(b * order, order), order)
+            peer_x(d),
+        )
+
+    def owner(j, d):
+        return at_z(d) * ys + 2 * core + j
+
+    def b_copy(s, j, d):
         return remote(
-            b_out.at[s, :, cols],
+            b_out.at[s, :, columns(j * chunk + at_z(d) * order, order)],
             b_in.at[s, blk],
-            b_s.at[s, b],
+            b_s.at[s, j, d],
             b_r.at[s, blk],
-            (dom, core * per_half + b),
-        )
-
-    def b_arrival(s, sender):
-        return remote(
-            b_out.at[s, :, pl.ds(0, order)],
-            b_in.at[s, sender],
-            b_s.at[s, 0],
-            b_r.at[s, sender],
-            (dom, sender),
-        )
-
-    def refl_at(s, b):
-        cols = pl.ds(pl.multiple_of((core * per_half + b) * order, order), order)
-        return refl.at[s, my_rows, cols]
-
-    mine = lax.rem(blk, per_half)
+            (dom, owner(j, d)),
+        )
+
+    def b_arrival(s, i):
+        return remote(b_in.at[s, i], b_in.at[s, i], b_s.at[s, 0, 0], b_r.at[s, i], (dom, i))
+
+    def block(s, rows, at_y, z_of):
+        return refl.at[s, rows, columns((at_y * zs + z_of) * order, order)]
 
     def a_copy(s, o):
-        return remote(
-            refl_at(s, mine),
-            refl_at(s, mine),
-            a_s.at[s, o],
-            a_r.at[s, mine],
-            (dom, lax.rem(blk + o, blks)),
-        )
-
-    def a_arrival(s, b):
-        return remote(
-            refl_at(s, b), refl_at(s, b), a_s.at[s, 0], a_r.at[s, b], (dom, core * per_half + b)
-        )
-
-    def x2_copy(s, d, b):
-        return remote(
-            refl_at(s, b),
-            refl_at(s, b),
-            x2_s.at[s, d - 1, b],
-            x2_r.at[s, d - 1, b],
-            (peer_x(d), blk),
-        )
-
-    def x2_arrival(s, d, b):
-        theirs = pl.ds(pl.multiple_of(lax.rem(x + xs - d, xs) * part, part), part)
-        cols = pl.ds(pl.multiple_of((core * per_half + b) * order, order), order)
-        place = refl.at[s, theirs, cols]
-        return remote(
-            place, place, x2_s.at[s, d - 1, b], x2_r.at[s, d - 1, b], (peer_x(xs - d), blk)
-        )
-
-    def p2_copy(s, j, sender):
-        cols = pl.ds(pl.multiple_of(sender * half + j * chunk, chunk), chunk)
-        return remote(
-            refl.at[s, :, cols], refl.at[s, :, cols], p2_s.at[s, j], p2_r.at[s, j], (partner, blk)
-        )
-
-    @pl.loop(0, ITERS)
-    def _(s):
+        here = block(s, x_rows(x), y, z)
+        sem = a_r.at[s, lax.rem(y, 2), z]
+        return remote(here, here, a_s.at[s, o], sem, (dom, lax.rem(blk + o, blks)))
+
+    def a_arrival(s, j, d):
+        here = block(s, x_rows(x), 2 * core + j, at_z(d))
+        return remote(here, here, a_s.at[s, 0], a_r.at[s, j, at_z(d)], (dom, owner(j, d)))
+
+    def x2_copy(s, j, d, e):
+        here = block(s, x_rows(x), 2 * core + j, at_z(e))
+        sem = (s, d - 1, j, at_z(e))
+        return remote(here, here, x2_s.at[sem], x2_r.at[sem], peer_x(d))
+
+    def x2_arrival(s, j, d, i):
+        here = block(s, x_rows(at_x(xs - d)), 2 * core + j, i)
+        sem = (s, d - 1, j, i)
+        return remote(here, here, x2_s.at[sem], x2_r.at[sem], peer_x(xs - d))
+
+    def p2_copy(s, d, sender):
+        here = refl.at[s, x_rows(at_x(xs - d)), pl.ds(pl.multiple_of(sender * half, half), half)]
+        return remote(here, here, p2_s.at[s, d], p2_r.at[s, d], (partner, blk))
+
+    def near_first(n):
+        return sorted(range(n), key=lambda d: (min(d, n - d), d))
+
+    def launch(s):
         @pl.loop(0, 2)
         def _(j):
-            cols = pl.ds(pl.multiple_of(j * chunk, chunk), chunk)
-            pair_out[s, :, cols] = outward((1 - core) * half + j * chunk).astype(BF16)
+            pair_out[s, :, chunk_cols(j)] = outward((1 - core) * half + j * chunk).astype(BF16)
             pair_copy(s, j).start()
 
         @pl.loop(0, 2)
         def _(j):
-            cols = pl.ds(pl.multiple_of(j * chunk, chunk), chunk)
+            cols = chunk_cols(j)
             own = outward(core * half + j * chunk)
             pair_copy(s, j).wait_recv()
             x_out[s, :, cols] = (own + pair_in[s, :, cols].astype(F32)).astype(BF16)
-            for d in range(1, xs):
+            for d in near_first(xs)[:0:-1]:
                 x_copy(s, j, d).start()
 
-        @pl.when(s == 0)
-        def _():
-            moves_load.wait()
-            grating_load.wait()
-
+    launch(0)
+    halo_send(0, 1)
+    moves_load.wait()
+    grating_load.wait()
+
+    @pl.loop(0, ITERS)
+    def _(s):
         near_field(s, 0)
 
-        @pl.loop(0, 2)
-        def _(j):
-            cols = pl.ds(pl.multiple_of(j * chunk, chunk), chunk)
-            both = x_out[s, my_rows, cols].astype(F32)
+        for j in range(2):
+            both = x_out[s, x_rows(x), chunk_cols(j)].astype(F32)
             for d in range(1, xs):
                 x_copy(s, j, d).wait_recv()
-                both = both + x_in[s, d - 1, :, cols].astype(F32)
-            b_out[s, :, cols] = both.astype(BF16)
-
-            @pl.loop(0, per_chunk)
-            def _(i):
-                b = j * per_chunk + i
-
-                @pl.when(core * per_half + b != blk)
+                both = both + x_in[s, d - 1, :, chunk_cols(j)].astype(F32)
+            b_out[s, :, chunk_cols(j)] = both.astype(BF16)
+            for d in near_first(zs)[::-1]:
+
+                @pl.when(owner(j, d) != blk)
                 def _():
-                    b_copy(s, b).start()
+                    b_copy(s, j, d).start()
 
         halo_send(s, 2)
         near_field(s, 1)
 
         @pl.when(is_owner)
         def _():
-            own_cols = pl.ds(pl.multiple_of(mine * order, order), order)
-
             def gather(o, so_far):
-                sender = lax.rem(blk + o, blks)
-                b_arrival(s, sender).wait_recv()
-                return so_far + b_in[s, sender].astype(F32)
-
-            sums = lax.fori_loop(1, blks, gather, b_out[s, :, own_cols].astype(F32))
+                i = lax.rem(blk + o, blks)
+                b_arrival(s, i).wait_recv()
+                return so_far + b_in[s, i].astype(F32)
+
+            own = b_out[s, :, columns(lax.rem(y, 2) * chunk + z * order, order)].astype(F32)
+            sums = lax.fori_loop(1, blks, gather, own)
             result = dot(sums, grating_ref[0], NT_DIMS, lax.Precision.HIGHEST)
-            out_cols = pl.ds(pl.multiple_of(blk * order, order), order)
-            refl[s, my_rows, out_cols] = result.astype(BF16)
+            refl[s, x_rows(x), columns((y * zs + z) * order, order)] = result.astype(BF16)
 
             @pl.loop(1, blks)
             def _(o):
@@ -416,51 +422,54 @@
         halo_send(s, 3)
         near_field(s, 2)
 
-        @pl.loop(0, per_half)
-        def _(o):
-            b = lax.rem(mine + o, per_half)
-
-            @pl.when(core * per_half + b != blk)
-            def _():
-                a_arrival(s, b).wait_recv()
-
-            for d in range(1, xs):
-                x2_copy(s, d, b).start()
+        for e in near_first(zs):
+            for j in range(2):
+
+                @pl.when(owner(j, e) != blk)
+                def _():
+                    a_arrival(s, j, e).wait_recv()
+
+                for d in near_first(xs)[:0:-1]:
+                    x2_copy(s, j, d, e).start()
+        p2_copy(s, 0, core).start()
 
         near_field(s, 3)
 
-        for j in range(2):
-
-            @pl.loop(0, per_chunk)
-            def _(i):
-                b = j * per_chunk + i
-                for d in range(1, xs):
-                    x2_arrival(s, d, b).wait_recv()
-
-            p2_copy(s, j, core).start()
-        for j in range(2):
-            inward(s, core * half + j * chunk, False)
-        for j in range(2):
-            p2_copy(s, j, 1 - core).wait_recv()
-            inward(s, (1 - core) * half + j * chunk, j == 1)
+        def inward_own(d):
+            inward(s, x_rows(at_x(xs - d)), core * half, False)
+
+        def inward_other(d):
+            p2_copy(s, d, 1 - core).wait_recv()
+            inward(s, x_rows(at_x(xs - d)), (1 - core) * half, True)
+
+        turn = near_first(xs)
+        inward_own(turn[0])
+        for n, d in enumerate(turn[1:]):
+            for j in range(2):
+                for i in range(zs):
+                    x2_arrival(s, j, d, i).wait_recv()
+            p2_copy(s, d, core).start()
+            inward_own(d)
+            inward_other(turn[n])
+        inward_other(turn[-1])
 
         for i in range(reach):
             halo_copy(s, i, True).wait_send()
             halo_copy(s, i, False).wait_send()
         for j in range(2):
             pair_copy(s, j).wait_send()
-            p2_copy(s, j, core).wait_send()
+            for d in range(zs):
+
+                @pl.when(owner(j, d) != blk)
+                def _():
+                    b_copy(s, j, d).wait_send()
+
             for d in range(1, xs):
                 x_copy(s, j, d).wait_send()
-
-        @pl.loop(0, per_half)
-        def _(b):
-            for d in range(1, xs):
-                x2_copy(s, d, b).wait_send()
-
-            @pl.when(core * per_half + b != blk)
-            def _():
-                b_copy(s, b).wait_send()
+                for e in range(zs):
+                    x2_copy(s, j, d, e).wait_send()
+        for d in range(xs):
+            p2_copy(s, d, core).wait_send()
 
         @pl.when(is_owner)
         def _():
@@ -475,22 +484,44 @@
                 win[reach + p] = dot(src[p], t_ref[p], NT_DIMS).astype(BF16)
                 return carry
 
-            lax.fori_loop(0, reach, solve_next, 0)
-            for batch in range(reach // 2):
-                halo_send(s + 1, batch)
-            lax.fori_loop(reach, count, solve_next, 0)
-
-    def out_copy(p):
-        return pltpu.make_async_copy(out_stage.at[p], out_hbm.at[p], out_sem.at[p])
+            lax.fori_loop(0, count - 2, solve_next, 0)
+            halo_send(s + 1, 0)
+            lax.fori_loop(count - 2, count, solve_next, 0)
+            launch(s + 1)
+            halo_send(s + 1, 1)
+
+    out = pltpu.make_async_copy(src, out_hbm, out_sem.at[0])
+    out.start()
+    out.wait()
+
+
+def last_solve(src_hbm, t_hbm, out_hbm, src, t_ref, out, src_sem, t_sem, out_sem):
+    count = src.shape[0]
+
+    def load(p):
+        return (
+            pltpu.make_async_copy(src_hbm.at[p], src.at[p], src_sem.at[p]),
+            pltpu.make_async_copy(t_hbm.at[p], t_ref.at[p], t_sem.at[p]),
+        )
+
+    def store(p):
+        return pltpu.make_async_copy(out.at[p], out_hbm.at[p], out_sem.at[p])
 
     @pl.loop(0, count)
     def _(p):
-        out_stage[p] = dot(src[p], t_ref[p], NT_DIMS).astype(BF16)
-        out_copy(p).start()
+        for copy in load(p):
+            copy.start()
 
     @pl.loop(0, count)
     def _(p):
-        out_copy(p).wait()
+        for copy in load(p):
+            copy.wait()
+        out[p] = dot(src[p], t_ref[p], NT_DIMS).astype(BF16)
+        store(p).start()
+
+    @pl.loop(0, count)
+    def _(p):
+        store(p).wait()
 
 
 def local(
@@ -506,6 +537,8 @@
 ):
     doms, blks = lax.axis_size("dom"), lax.axis_size("blk")
     xs = doms // 2
+    zs = xs
+    ys = blks // zs
     count, width, rows_m = incident.shape
     turned = (count, rows_m, width)
     reach = count // 2
@@ -513,15 +546,15 @@
     most = near_index.shape[1]
     total = wave_basis.shape[0]
     half = total // 2
+    chunk = half // 2
     order = grating_blocks.shape[1]
     part = rows_m // xs
-    per_half = blks // 2
     hbm = pl.BlockSpec(memory_space=pl.ANY)
     smem = pl.BlockSpec(memory_space=pltpu.SMEM)
     sem = pltpu.SemaphoreType.DMA
     n = ITERS
-    result = pl.pallas_call(
-        functools.partial(kernel, xs),
+    source = pl.pallas_call(
+        functools.partial(kernel, xs, zs),
         out_shape=jax.ShapeDtypeStruct(turned, BF16),
         in_specs=[smem] * 3 + [hbm] * 6,
         out_specs=hbm,
@@ -530,7 +563,6 @@
             pltpu.VMEM((count, total), BF16),
             pltpu.VMEM((count, 1, total), BF16),
             pltpu.VMEM((1, order, order), F32),
-            pltpu.VMEM(turned, BF16),
             pltpu.VMEM(turned, BF16),
             pltpu.VMEM((count, width, width), BF16),
             pltpu.VMEM((kinds, width, width), BF16),
@@ -551,19 +583,20 @@
             sem((count,)),
             sem((count,)),
             sem((4,)),
-            sem((count,)),
+            sem((blks,)),
+            sem((1,)),
             sem((n, 2)),
             sem((n, 2)),
             sem((n, 2, xs - 1)),
             sem((n, 2, xs - 1)),
-            sem((n, per_half)),
+            sem((n, 2, zs)),
             sem((n, blks)),
             sem((n, blks)),
-            sem((n, per_half)),
-            sem((n, xs - 1, per_half)),
-            sem((n, xs - 1, per_half)),
-            sem((n, 2)),
-            sem((n, 2)),
+            sem((n, 2, zs)),
+            sem((n, xs - 1, 2, zs)),
+            sem((n, xs - 1, 2, zs)),
+            sem((n, xs)),
+            sem((n, xs)),
             sem((n, 2 * reach)),
             sem((n, 2 * reach)),
         ],
@@ -581,6 +614,21 @@
         wave_basis,
         grating_blocks,
     )
+    result = pl.pallas_call(
+        last_solve,
+        out_shape=jax.ShapeDtypeStruct(turned, BF16),
+        in_specs=[hbm] * 2,
+        out_specs=hbm,
+        scratch_shapes=[
+            pltpu.VMEM(turned, BF16),
+            pltpu.VMEM((count, width, width), BF16),
+            pltpu.VMEM(turned, BF16),
+            sem((count,)),
+            sem((count,)),
+            sem((count,)),
+        ],
+        compiler_params=pltpu.CompilerParams(vmem_limit_bytes=60 * 2**20),
+    )(source, t_matrices)
     return jnp.swapaxes(result, 1, 2)
 
 

time: 85.4 us -> 84.7 us (level)
  local copies, waits for them, and re-layouts: 2.65 us -> 0 us
  Pallas kernels: 82.6 us -> 83.7 us
    unnamed x1 -> x0, local copies, waits for them, and re-layouts: 2.65 us -> none
    pallas_call x1 -> x2, Pallas kernels: 82.6 us -> 83.7 us  [the longest x1 79 us: local(): pl.pallas_call(functools.partial(kernel, xs, zs), out_shape=jax.ShapeDtyp...]
where the time goes in v3:
time: 84.7 us; the launch traced here: 83.7 us
  Pallas kernels  83.7 us (99%)
    pallas_call x1, Pallas kernels, local(): pl.pallas_call(functools.partial(kernel, xs, zs), out_shape=jax.ShapeDtyp...  79 us
    pallas_call x1, Pallas kernels, local(): pl.pallas_call(last_solve, out_shape=jax.ShapeDtypeStruct(turned, BF16),...  4.67 us

profile of v3, /device:TPU:0, one launch (start us, length us, event | category | flops | bytes accessed | tf_op | source)
XLA Modules:
  0.0 83.7 jit_solution(9517887846099889353)
XLA Ops:
  0.0 79.0 %shard_map.91.src_hbm = bf16[8,192,512]{2,1,0:T(8,128)(2,1)} custom-call(s32[8,6]{1,0:T(8,128)} %index_ref.1, s32[8]{0:T(128)} %count_ref.1, s32[8,6]{1,0:T(8,128)} %type_ref.1, bf16[8,192,512]{2,1,0:T(8,128)(2,1)} %bitcast.2, bf16[8,512,512]{2,1,0:T(8,128)(2,1)} %t_hbm.3, bf16[4,512,512]{2,1,0:T(8,128)(2,1)} %moves_hbm.1, bf16[8,2048]{1,0:T(8,128)(2,1)} %phases_hbm.1, ...), custom_call_target="tpu_custom_call" | custom-call | tf_op jit(solution)/shard_map/pallas_call | solution.py:556
  79.0 4.7 %shard_map.92 = bf16[8,192,512]{2,1,0:T(8,128)(2,1)} custom-call(bf16[8,192,512]{2,1,0:T(8,128)(2,1)} %shard_map.91.src_hbm, bf16[8,512,512]{2,1,0:T(8,128)(2,1)} %t_hbm.3), custom_call_target="tpu_custom_call" | custom-call | tf_op jit(solution)/shard_map/pallas_call | solution.py:617

commit v4 on v3

--- a/solution.py
+++ b/solution.py
@@ -456,6 +456,19 @@
         for i in range(reach):
             halo_copy(s, i, True).wait_send()
             halo_copy(s, i, False).wait_send()
+        @pl.when(s < ITERS - 1)
+        def _():
+            def solve_next(i, carry):
+                p = solve_order(i)
+                win[reach + p] = dot(src[p], t_ref[p], NT_DIMS).astype(BF16)
+                return carry
+
+            lax.fori_loop(0, count - 2, solve_next, 0)
+            halo_send(s + 1, 0)
+            lax.fori_loop(count - 2, count, solve_next, 0)
+            launch(s + 1)
+            halo_send(s + 1, 1)
+
         for j in range(2):
             pair_copy(s, j).wait_send()
             for d in range(zs):
@@ -476,19 +489,6 @@
             @pl.loop(1, blks)
             def _(o):
                 a_copy(s, o).wait_send()
-
-        @pl.when(s < ITERS - 1)
-        def _():
-            def solve_next(i, carry):
-                p = solve_order(i)
-                win[reach + p] = dot(src[p], t_ref[p], NT_DIMS).astype(BF16)
-                return carry
-
-            lax.fori_loop(0, count - 2, solve_next, 0)
-            halo_send(s + 1, 0)
-            lax.fori_loop(count - 2, count, solve_next, 0)
-            launch(s + 1)
-            halo_send(s + 1, 1)
 
     out = pltpu.make_async_copy(src, out_hbm, out_sem.at[0])
     out.start()

time: 84.7 us -> 85.8 us (1.013)
  Pallas kernels: 83.7 us -> 84.8 us
    pallas_call x1, Pallas kernels: 79 us -> 80.1 us  [local(): pl.pallas_call(functools.partial(kernel, xs, zs), out_shape=jax.ShapeDtyp...]
where the time goes in v4:
time: 85.8 us; the launch traced here: 84.8 us
  Pallas kernels  84.8 us (99%)
    pallas_call x1, Pallas kernels, local(): pl.pallas_call(functools.partial(kernel, xs, zs), out_shape=jax.ShapeDtyp...  80.1 us
    pallas_call x1, Pallas kernels, local(): pl.pallas_call(last_solve, out_shape=jax.ShapeDtypeStruct(turned, BF16),...  4.67 us

profile of v4, /device:TPU:0, one launch (start us, length us, event | category | flops | bytes accessed | tf_op | source)
XLA Modules:
  0.0 84.8 jit_solution(3332857273120196076)
XLA Ops:
  0.0 80.1 %shard_map.91.src_hbm = bf16[8,192,512]{2,1,0:T(8,128)(2,1)} custom-call(s32[8,6]{1,0:T(8,128)} %index_ref.1, s32[8]{0:T(128)} %count_ref.1, s32[8,6]{1,0:T(8,128)} %type_ref.1, bf16[8,192,512]{2,1,0:T(8,128)(2,1)} %bitcast.2, bf16[8,512,512]{2,1,0:T(8,128)(2,1)} %t_hbm.3, bf16[4,512,512]{2,1,0:T(8,128)(2,1)} %moves_hbm.1, bf16[8,2048]{1,0:T(8,128)(2,1)} %phases_hbm.1, ...), custom_call_target="tpu_custom_call" | custom-call | tf_op jit(solution)/shard_map/pallas_call | solution.py:556
  80.1 4.7 %shard_map.92 = bf16[8,192,512]{2,1,0:T(8,128)(2,1)} custom-call(bf16[8,192,512]{2,1,0:T(8,128)(2,1)} %shard_map.91.src_hbm, bf16[8,512,512]{2,1,0:T(8,128)(2,1)} %t_hbm.3), custom_call_target="tpu_custom_call" | custom-call | tf_op jit(solution)/shard_map/pallas_call | solution.py:617
